TPU v7x, 256 devices: a whole 4x4x8 slice. The times are simulated.
256 devices in a mesh: row: 32 (over x_lo, z, core), col: 8 (over y, x_hi).
Axes of the slice: x: 4 (x_hi: 2, x_lo: 2; x = x_hi * 2 + x_lo), y: 4, z: 8, core: 2. Of those that a mesh axis runs over, the one named last changes fastest.
Arguments:
- corr: float32 [2, 8192, 8192], P(None, 'row', 'col'), may hold values from -6 to 6
- slope_prev: float32 [2, 8192, 8192], P(None, 'row', 'col'), may hold values from -6 to 6
- kappa: float32 [8192], replicated, may hold values from 0.05 to 0.2
- detuning: float32 [8192], replicated, may hold values from -1 to 1
- pump: float32 [8192], replicated, may hold values from 0.5 to 2
- round_trip: float32 [2], replicated, may hold values from -0.6 to 0.6
Outputs:
- slope: float32 [2, 8192, 8192], P(None, 'row', 'col')
All inputs are finite; a program needn't handle non-finite values.
Results may differ from a plain program's by a relative error of at most 0.00005.
Values sent between devices are 32-bit elements; how exact they have to be, the bound alone decides.
No kernel may reach another device: no remote copies, remote signals or barrier semaphores. Data moves between devices by JAX's collectives and lax.ppermute only.
A program may use at most 64 MiB of HBM per device.

v0:
```python
import jax
import jax.numpy as jnp
from jax import lax
from jax.sharding import PartitionSpec as P


def carried_in(x, axis, combine, identity):
    devices, here = (lax.axis_size(axis), lax.axis_index(axis))
    everything = lax.all_gather(x, axis)
    start = jnp.broadcast_to(jnp.asarray(identity, x.dtype), x.shape)

    def lap(k, before):
        reached = k < here
        new = combine(before, everything[k])
        return jnp.where(reached, new, before)

    return lax.fori_loop(0, devices, lap, start)


def lower_table(width):
    above = lax.broadcasted_iota(jnp.int32, (width, width), 0)
    beside = lax.broadcasted_iota(jnp.int32, (width, width), 1)
    return (above > beside).astype(jnp.float32)


def rows_prefix(part):
    count = part.shape[1]
    width = min(128, count)
    blocks = part.reshape(2, count // width, width, part.shape[2])
    within = jnp.einsum(
        "ij,pbjc->pbic", lower_table(width), blocks, precision=lax.Precision.HIGHEST
    )
    sums = jnp.sum(blocks, axis=2)
    earlier = jnp.cumsum(sums, axis=1) - sums
    return ((within + earlier[:, :, None, :]).reshape(part.shape), jnp.sum(sums, axis=1))


def cols_prefix(part):
    count = part.shape[2]
    width = min(128, count)
    blocks = part.reshape(2, part.shape[1], count // width, width)
    within = jnp.einsum(
        "prbj,ij->prbi", blocks, lower_table(width), precision=lax.Precision.HIGHEST
    )
    sums = jnp.sum(blocks, axis=3)
    earlier = jnp.cumsum(sums, axis=2) - sums
    return ((within + earlier[:, :, :, None]).reshape(part.shape), jnp.sum(sums, axis=2))


def add_pair(earlier, later):
    return earlier + later


def shards(corr, slope_prev, kappa, detuning, pump, round_trip):
    rows = corr.shape[1]
    cols = corr.shape[2]
    row_start = lax.axis_index("row") * rows
    col_start = lax.axis_index("col") * cols
    kappa_rows = lax.dynamic_slice_in_dim(kappa, row_start, rows)
    kappa_cols = lax.dynamic_slice_in_dim(kappa, col_start, cols)
    detune_rows = lax.dynamic_slice_in_dim(detuning, row_start, rows)
    detune_cols = lax.dynamic_slice_in_dim(detuning, col_start, cols)
    pump_rows = lax.dynamic_slice_in_dim(pump, row_start, rows)
    rho_re = round_trip[0]
    rho_im = round_trip[1]
    section = corr + 0.25 * slope_prev
    upper = section * kappa_rows[None, :, None]
    weighted = section * kappa_cols[None, None, :]
    local_rows, own_rows = rows_prefix(upper)
    local_cols, own_cols = cols_prefix(weighted)
    dev_rows = carried_in(own_rows, "row", add_pair, jnp.zeros_like(own_rows))
    dev_cols = carried_in(own_cols, "col", add_pair, jnp.zeros_like(own_cols))
    later_rows = lax.psum(own_rows, "row") - dev_rows - own_rows
    later_cols = lax.psum(own_cols, "col") - dev_cols - own_cols
    before = local_rows + dev_rows[:, None, :]
    after = later_rows[:, None, :] + (own_rows[:, None, :] - local_rows - upper)
    turned = jnp.stack(
        [rho_re * after[0] - rho_im * after[1], rho_re * after[1] + rho_im * after[0]]
    )
    field_left = -kappa_rows[None, :, None] * (before + 0.5 * upper + turned)
    before = local_cols + dev_cols[:, :, None]
    after = later_cols[:, :, None] + (own_cols[:, :, None] - local_cols - weighted)
    turned = jnp.stack(
        [rho_re * after[0] + rho_im * after[1], rho_re * after[1] - rho_im * after[0]]
    )
    field_right = -kappa_cols[None, None, :] * (before + 0.5 * weighted + turned)
    gap = detune_cols[None, :] - detune_rows[:, None]
    spin = jnp.stack([-gap * section[1], gap * section[0]])
    global_rows = row_start + lax.broadcasted_iota(jnp.int32, (rows, cols), 0)
    global_cols = col_start + lax.broadcasted_iota(jnp.int32, (rows, cols), 1)
    source = jnp.where(global_rows == global_cols, pump_rows[:, None], 0.0)
    source = jnp.stack([source, jnp.zeros_like(source)])
    return field_left + field_right + spin + source


def solution(mesh):
    placed = (P(None, "row", "col"), P(None, "row", "col"), P(), P(), P(), P())
    return jax.shard_map(
        shards, mesh=mesh, in_specs=placed, out_specs=P(None, "row", "col"), check_vma=False
    )
```

profile of v0, /device:TPU:1, one launch (start us, length us, event | category | flops | bytes accessed | tf_op | source)
XLA Modules:
  0.0 175.6 jit_solution(7867016755998997292)
XLA Ops:
  0.0 0.7 fusion.19
  0.7 3.8 %fusion.20 = (f32[2,256]{1,0:T(2,128)S(1)}, f32[2,256,1024]{2,1,0:T(8,128)S(1)}, f32[2,256,1024]{2,1,0:T(8,128)}) fusion(f32[1024]{0:T(1024)S(1)} %get-tuple-element.214, f32[2,256,1024]{2,1,0:T(8,128)} %param.10, f32[2,256,1024]{2,1,0:T(8,128)} %param.11), kind=kLoop, calls=%fused_computation.41 | loop fusion | flops 2096640 | bytes 8394752 | tf_op jit(solution)/shard_map/reduce_sum | solution.py:47
  4.5 0.0 copy-start
  4.5 0.5 copy.16
  5.0 0.6 bitcast_reduce_fusion
  5.6 0.4 reduce_window_sum.23
  6.1 0.1 copy.11
  6.2 2.6 %fusion.11 = f32[2,256,8,128]{1,3,2,0:T(8,128)} fusion(f32[2,256,8]{1,2,0:T(8,128)S(1)} %copy.11, f32[2,256,1024]{2,1,0:T(8,128)S(1)} %get-tuple-element.216), kind=kOutput, calls=%fused_computation.20 | convolution fusion | flops 805847040 | bytes 4210688 | tf_op jit(solution)/shard_map/prbj,ij->prbi/dot_general | solution.py:42
  8.8 2.9 %copy.12 = f32[2,256,1024]{2,1,0:T(8,128)} copy(f32[2,256,1024]{1,2,0:T(8,128)} %bitcast.52) | data formatting | bytes 4194304 | tf_op jit(solution)/shard_map/reshape | solution.py:47
  11.6 26.4 %all-gather.3 = f32[8,2,256]{2,1,0:T(2,128)S(1)} all-gather(f32[1,2,256]{2,1,0:T(2,128)S(1)} %bitcast.55), channel_id=3, replica_groups=mesh['row'=32,'col'=8] {'col'}, dimensions={0}, use_global_device_ids=true | all-gather | bytes 18432 | tf_op jit(solution)/shard_map/all_gather | solution.py:9
  38.0 0.3 while.29
  38.3 19.5 %psum.15 = f32[2,256]{1,0:T(2,128)S(1)} all-reduce(f32[2,256]{1,0:T(2,128)S(1)} %get-tuple-element.215), channel_id=1, replica_groups=mesh['row'=32,'col'=8] {'col'}, use_global_device_ids=true, to_apply=%region_11.12 | all-reduce | flops 512 | bytes 4096 | tf_op jit(solution)/shard_map/psum | solution.py:74
  57.8 0.0 copy-done
  57.8 0.0 copy-start.6
  57.8 1.9 %subtract_add_fusion = f32[2,256,1024]{2,1,0:T(8,128)S(1)} fusion(f32[2,256,1024]{2,1,0:T(8,128)S(1)} %get-tuple-element.216, f32[2,256,1024]{2,1,0:T(8,128)} %copy.12, f32[2,256]{1,0:T(2,128)S(1)} %get-tuple-element.215, f32[2,256]{1,0:T(2,128)S(1)} %subtract_subtract_fusion.1), kind=kLoop, calls=%fused_computation.18 | loop fusion | flops 1572864 | bytes 6295552 | tf_op jit(solution)/shard_map/add | solution.py:82
  59.8 0.0 copy-done.6
  59.8 0.6 fusion.22
  60.4 2.5 %multiply_add_fusion.1 = (f32[1,256,1024]{2,1,0:T(8,128)S(1)}, f32[1,256,1024]{2,1,0:T(8,128)}) fusion(f32[2,256,1024]{2,1,0:T(8,128)S(1)} %subtract_add_fusion, f32[]{:T(128)} %bitcast.8, f32[]{:T(128)} %bitcast.6), kind=kLoop, calls=%fused_computation.26 | loop fusion | flops 1572864 | bytes 4194312 | tf_op jit(solution)/shard_map/add | solution.py:84
  63.0 0.8 fusion.18
  63.7 1.8 %fusion.21 = (f32[2,1024]{1,0:T(2,128)S(1)}, f32[2,256,1024]{2,1,0:T(8,128)S(1)}) fusion(f32[2,256,1024]{2,1,0:T(8,128)} %get-tuple-element.217, f32[256]{0:T(256)S(1)} %get-tuple-element.212), kind=kLoop, calls=%fused_computation.42 | loop fusion | flops 1046528 | bytes 4203520 | tf_op jit(solution)/shard_map/reduce_sum | solution.py:35
  65.6 46.4 %all-gather.2 = f32[32,2,1024]{2,1,0:T(2,128)S(1)} all-gather(f32[1,2,1024]{2,1,0:T(2,128)S(1)} %bitcast.54), channel_id=2, replica_groups=mesh['row'=32,'col'=8] {'row'}, dimensions={0}, use_global_device_ids=true | all-gather | bytes 270336 | tf_op jit(solution)/shard_map/all_gather | solution.py:9
  112.0 1.3 while.28
  113.3 53.5 %psum.14 = f32[2,1024]{1,0:T(2,128)S(1)} all-reduce(f32[2,1024]{1,0:T(2,128)S(1)} %get-tuple-element.218), channel_id=1, replica_groups=mesh['row'=32,'col'=8] {'row'}, use_global_device_ids=true, to_apply=%region_5.6 | all-reduce | flops 2048 | bytes 16384 | tf_op jit(solution)/shard_map/psum | solution.py:73
  166.8 0.2 bitcast_reduce_fusion.1
  167.0 0.1 reduce_window_sum.22
  167.1 1.4 convolution_add_fusion
  168.5 0.5 fusion.10
  168.9 0.0 copy-start.5
  168.9 0.0 copy-start.3
  168.9 0.0 dynamic-slice-start
  169.0 1.7 multiply_subtract_fusion.1
  170.7 0.0 copy-done.5
  170.7 0.1 dynamic_slice.32
  170.8 0.0 copy-done.3
  170.8 0.0 dynamic-slice-done
  170.8 0.0 copy-start.1
  170.8 0.0 copy-start.2
  170.8 0.0 copy-start.4
  170.8 0.2 fusion.14
  171.0 0.9 dynamic_slice.33
  171.9 0.2 compare_select_fusion
  172.1 0.3 copy-done.1
  172.4 0.6 copy-done.2
  173.0 0.3 copy-done.4
  173.3 2.3 %fusion.6 = f32[2,256,1024]{2,1,0:T(8,128)} fusion(f32[1,256,1024]{2,1,0:T(8,128)S(1)} %get-tuple-element.225, f32[1,256,1024]{2,1,0:T(8,128)S(1)} %get-tuple-element.224, f32[1,256,1024]{2,1,0:T(8,128)S(1)} %copy-done.4, f32[1,256,1024]{2,1,0:T(8,128)S(1)} %get-tuple-element.222, f32[1,256,1024]{2,1,0:T(8,128)S(1)} %get-tuple-element.221, ...), kind=kLoop, calls=%fused_computation.10 | loop fusion | flops 8388608 | bytes 17841152 | tf_op jit(solution)/shard_map/add | solution.py:93
  (48 shorter events, 0.7 us)
Async XLA Ops:
  4.5 53.3 %copy-start = (f32[2,256,1024]{2,1,0:T(8,128)}, f32[2,256,1024]{2,1,0:T(8,128)S(1)}, u32[]{:S(2)}) copy-start(f32[2,256,1024]{2,1,0:T(8,128)S(1)} %get-tuple-element.216) | copy-start | bytes 6291460
  57.8 1.9 %copy-start.6 = (f32[2]{0:T(128)S(1)}, f32[2]{0:T(128)}, u32[]{:S(2)}) copy-start(f32[2]{0:T(128)} %param.15) | copy-start | bytes 28
  168.9 1.7 copy-start.5
  168.9 1.8 %copy-start.3 = (f32[2,256,1024]{2,1,0:T(8,128)S(1)}, f32[2,256,1024]{2,1,0:T(8,128)}, u32[]{:S(2)}) copy-start(f32[2,256,1024]{2,1,0:T(8,128)} %get-tuple-element.217) | copy-start | bytes 6291460
  168.9 1.8 %dynamic-slice-start = ((f32[8192]{0:T(1024)}, s32[]{:T(128)}), f32[1024]{0:T(1024)S(1)}, s32[]{:S(2)}) async-start(f32[8192]{0:T(1024)} %param.13, s32[]{:T(128)} %select_n.63), calls=%async_computation | async-start | bytes 8704 | tf_op jit(solution)/shard_map/dynamic_slice | solution.py:62
  170.8 1.6 copy-start.1
  170.8 2.2 %copy-start.2 = (f32[2,256,1024]{2,1,0:T(8,128)S(1)}, f32[2,256,1024]{2,1,0:T(8,128)}, u32[]{:S(2)}) copy-start(f32[2,256,1024]{2,1,0:T(8,128)} %copy.12) | copy-start | bytes 6291460
  170.8 2.5 %copy-start.4 = (f32[1,256,1024]{2,1,0:T(8,128)S(1)}, f32[1,256,1024]{2,1,0:T(8,128)}, u32[]{:S(2)}) copy-start(f32[1,256,1024]{2,1,0:T(8,128)} %get-tuple-element.223) | copy-start | bytes 3145732
where the time goes:
time: 176 us
  blocking collectives  146 us (83%)
  other arithmetic  18.4 us (10%)
  local copies, waits for them, and re-layouts  6.32 us (4%)
  matrix products  3.93 us (2%)
    all_gather x2, blocking collectives, carried_in(): everything = lax.all_gather(x, axis)  72.8 us
    psum x1, blocking collectives, shards(): later_rows = lax.psum(own_rows, 'row') - dev_rows - own_rows  53.5 us
    psum x1, blocking collectives, shards(): later_cols = lax.psum(own_cols, 'col') - dev_cols - own_cols  19.5 us
    reduce_sum x1, other arithmetic, cols_prefix(): jnp.sum(sums, axis=2)  3.83 us

commit v1 on v0

--- a/solution.py
+++ b/solution.py
@@ -1,7 +1,15 @@
+import functools
 import jax
 import jax.numpy as jnp
 from jax import lax
 from jax.sharding import PartitionSpec as P
+
+
+def pipes_push(v0, axis_name):
+    return jnp.sum(lax.all_gather(v0, axis_name), axis=0)
+
+
+update_fields_here = functools.partial(pipes_push, axis_name="col")
 
 
 def carried_in(x, axis, combine, identity):
@@ -71,7 +79,7 @@
     dev_rows = carried_in(own_rows, "row", add_pair, jnp.zeros_like(own_rows))
     dev_cols = carried_in(own_cols, "col", add_pair, jnp.zeros_like(own_cols))
     later_rows = lax.psum(own_rows, "row") - dev_rows - own_rows
-    later_cols = lax.psum(own_cols, "col") - dev_cols - own_cols
+    later_cols = update_fields_here(own_cols) - dev_cols - own_cols
     before = local_rows + dev_rows[:, None, :]
     after = later_rows[:, None, :] + (own_rows[:, None, :] - local_rows - upper)
     turned = jnp.stack(

time: 176 us -> 154 us (0.88)
  blocking collectives: 146 us -> 124 us
    psum x1 -> x0, blocking collectives: 19.5 us -> none  [shards(): later_cols = lax.psum(own_cols, 'col') - dev_cols - own_cols]
    all_gather x2, blocking collectives: 72.8 us -> 70.2 us  [carried_in(): everything = lax.all_gather(x, axis)]
where the time goes in v1:
time: 154 us
  blocking collectives  124 us (81%)
  other arithmetic  18.4 us (12%)
  local copies, waits for them, and re-layouts  6.32 us (4%)
  matrix products  3.93 us (3%)
    all_gather x2, blocking collectives, carried_in(): everything = lax.all_gather(x, axis)  70.2 us
    psum x1, blocking collectives, shards(): later_rows = lax.psum(own_rows, 'row') - dev_rows - own_rows  53.5 us
    reduce_sum x1, other arithmetic, cols_prefix(): jnp.sum(sums, axis=2)  3.83 us

profile of v1, /device:TPU:1, one launch (start us, length us, event | category | flops | bytes accessed | tf_op | source)
XLA Modules:
  0.0 153.5 jit_solution(11494048680140368194)
XLA Ops:
  0.0 0.7 fusion.19
  0.7 3.8 %fusion.20 = (f32[2,256]{1,0:T(2,128)S(1)}, f32[2,256,1024]{2,1,0:T(8,128)S(1)}, f32[2,256,1024]{2,1,0:T(8,128)}) fusion(f32[1024]{0:T(1024)S(1)} %get-tuple-element.214, f32[2,256,1024]{2,1,0:T(8,128)} %param.10, f32[2,256,1024]{2,1,0:T(8,128)} %param.11), kind=kLoop, calls=%fused_computation.41 | loop fusion | flops 2096640 | bytes 8394752 | tf_op jit(solution)/shard_map/reduce_sum | solution.py:55
  4.5 0.0 copy-start
  4.5 0.5 copy.16
  5.0 0.6 bitcast_reduce_fusion
  5.6 0.4 reduce_window_sum.23
  6.1 0.1 copy.11
  6.2 2.6 %fusion.11 = f32[2,256,8,128]{1,3,2,0:T(8,128)} fusion(f32[2,256,8]{1,2,0:T(8,128)S(1)} %copy.11, f32[2,256,1024]{2,1,0:T(8,128)S(1)} %get-tuple-element.216), kind=kOutput, calls=%fused_computation.20 | convolution fusion | flops 805847040 | bytes 4210688 | tf_op jit(solution)/shard_map/prbj,ij->prbi/dot_general | solution.py:50
  8.8 2.9 %copy.12 = f32[2,256,1024]{2,1,0:T(8,128)} copy(f32[2,256,1024]{1,2,0:T(8,128)} %bitcast.52) | data formatting | bytes 4194304 | tf_op jit(solution)/shard_map/reshape | solution.py:55
  11.6 26.4 %all-gather.3 = f32[8,2,256]{2,1,0:T(2,128)S(1)} all-gather(f32[1,2,256]{2,1,0:T(2,128)S(1)} %bitcast.55), channel_id=3, replica_groups=mesh['row'=32,'col'=8] {'col'}, dimensions={0}, use_global_device_ids=true | all-gather | bytes 18432 | tf_op jit(solution)/shard_map/all_gather | solution.py:17
  38.0 0.3 while.29
  38.3 0.0 copy-done
  38.4 0.0 copy-start.6
  38.4 1.9 %subtract_add_fusion = f32[2,256,1024]{2,1,0:T(8,128)S(1)} fusion(f32[2,256,1024]{2,1,0:T(8,128)S(1)} %get-tuple-element.216, f32[2,256,1024]{2,1,0:T(8,128)} %copy.12, f32[2,256]{1,0:T(2,128)S(1)} %get-tuple-element.215, f32[2,256]{1,0:T(2,128)S(1)} %subtract_subtract_fusion.1), kind=kLoop, calls=%fused_computation.18 | loop fusion | flops 1572864 | bytes 6295552 | tf_op jit(solution)/shard_map/add | solution.py:90
  40.3 0.0 copy-done.6
  40.3 0.6 fusion.22
  41.0 2.5 %multiply_add_fusion.1 = (f32[1,256,1024]{2,1,0:T(8,128)S(1)}, f32[1,256,1024]{2,1,0:T(8,128)}) fusion(f32[2,256,1024]{2,1,0:T(8,128)S(1)} %subtract_add_fusion, f32[]{:T(128)} %bitcast.8, f32[]{:T(128)} %bitcast.6), kind=kLoop, calls=%fused_computation.26 | loop fusion | flops 1572864 | bytes 4194312 | tf_op jit(solution)/shard_map/add | solution.py:92
  43.5 0.8 fusion.18
  44.2 1.8 %fusion.21 = (f32[2,1024]{1,0:T(2,128)S(1)}, f32[2,256,1024]{2,1,0:T(8,128)S(1)}) fusion(f32[2,256,1024]{2,1,0:T(8,128)} %get-tuple-element.217, f32[256]{0:T(256)S(1)} %get-tuple-element.212), kind=kLoop, calls=%fused_computation.42 | loop fusion | flops 1046528 | bytes 4203520 | tf_op jit(solution)/shard_map/reduce_sum | solution.py:43
  46.1 43.8 %all-gather.2 = f32[32,2,1024]{2,1,0:T(2,128)S(1)} all-gather(f32[1,2,1024]{2,1,0:T(2,128)S(1)} %bitcast.54), channel_id=2, replica_groups=mesh['row'=32,'col'=8] {'row'}, dimensions={0}, use_global_device_ids=true | all-gather | bytes 270336 | tf_op jit(solution)/shard_map/all_gather | solution.py:17
  89.9 1.3 while.28
  91.3 53.5 %psum.7 = f32[2,1024]{1,0:T(2,128)S(1)} all-reduce(f32[2,1024]{1,0:T(2,128)S(1)} %get-tuple-element.218), channel_id=1, replica_groups=mesh['row'=32,'col'=8] {'row'}, use_global_device_ids=true, to_apply=%region_5.6 | all-reduce | flops 2048 | bytes 16384 | tf_op jit(solution)/shard_map/psum | solution.py:81
  144.8 0.2 bitcast_reduce_fusion.1
  144.9 0.1 reduce_window_sum.22
  145.0 1.4 convolution_add_fusion
  146.4 0.5 fusion.10
  146.9 0.0 copy-start.5
  146.9 0.0 copy-start.3
  146.9 0.0 dynamic-slice-start
  146.9 1.7 %multiply_subtract_fusion.1 = (f32[1,256,1024]{2,1,0:T(8,128)S(1)}, f32[1,256,1024]{2,1,0:T(8,128)S(1)}) fusion(f32[2,256,1024]{2,1,0:T(8,128)S(1)} %fusion.10, f32[]{:T(128)} %bitcast.8, f32[]{:T(128)} %bitcast.6), kind=kLoop, calls=%fused_computation.29 | loop fusion | flops 1572864 | bytes 4194312 | tf_op jit(solution)/shard_map/sub | solution.py:86
  148.6 0.0 copy-done.5
  148.6 0.1 dynamic_slice.32
  148.7 0.0 copy-done.3
  148.7 0.0 dynamic-slice-done
  148.7 0.0 copy-start.1
  148.7 0.0 copy-start.2
  148.7 0.0 copy-start.4
  148.7 0.2 fusion.14
  149.0 0.9 dynamic_slice.33
  149.9 0.2 compare_select_fusion
  150.0 0.3 copy-done.1
  150.3 0.6 copy-done.2
  151.0 0.3 copy-done.4
  151.2 2.3 %fusion.6 = f32[2,256,1024]{2,1,0:T(8,128)} fusion(f32[1,256,1024]{2,1,0:T(8,128)S(1)} %get-tuple-element.225, f32[1,256,1024]{2,1,0:T(8,128)S(1)} %get-tuple-element.224, f32[1,256,1024]{2,1,0:T(8,128)S(1)} %copy-done.4, f32[1,256,1024]{2,1,0:T(8,128)S(1)} %get-tuple-element.222, f32[1,256,1024]{2,1,0:T(8,128)S(1)} %get-tuple-element.221, ...), kind=kLoop, calls=%fused_computation.10 | loop fusion | flops 8388608 | bytes 17841152 | tf_op jit(solution)/shard_map/add | solution.py:101
  (49 shorter events, 0.8 us)
Async XLA Ops:
  4.5 33.8 %copy-start = (f32[2,256,1024]{2,1,0:T(8,128)}, f32[2,256,1024]{2,1,0:T(8,128)S(1)}, u32[]{:S(2)}) copy-start(f32[2,256,1024]{2,1,0:T(8,128)S(1)} %get-tuple-element.216) | copy-start | bytes 6291460
  38.4 1.9 %copy-start.6 = (f32[2]{0:T(128)S(1)}, f32[2]{0:T(128)}, u32[]{:S(2)}) copy-start(f32[2]{0:T(128)} %param.15) | copy-start | bytes 28
  146.9 1.7 %copy-start.5 = (f32[8192]{0:T(1024)S(1)}, f32[8192]{0:T(1024)}, u32[]{:S(2)}) copy-start(f32[8192]{0:T(1024)} %param.13) | copy-start | bytes 98308
  146.9 1.8 %copy-start.3 = (f32[2,256,1024]{2,1,0:T(8,128)S(1)}, f32[2,256,1024]{2,1,0:T(8,128)}, u32[]{:S(2)}) copy-start(f32[2,256,1024]{2,1,0:T(8,128)} %get-tuple-element.217) | copy-start | bytes 6291460
  146.9 1.8 %dynamic-slice-start = ((f32[8192]{0:T(1024)}, s32[]{:T(128)}), f32[1024]{0:T(1024)S(1)}, s32[]{:S(2)}) async-start(f32[8192]{0:T(1024)} %param.13, s32[]{:T(128)} %select_n.63), calls=%async_computation | async-start | bytes 8704 | tf_op jit(solution)/shard_map/dynamic_slice | solution.py:70
  148.7 1.6 %copy-start.1 = (f32[2,256,1024]{2,1,0:T(8,128)S(1)}, f32[2,256,1024]{2,1,0:T(8,128)}, u32[]{:S(2)}) copy-start(f32[2,256,1024]{2,1,0:T(8,128)} %copy-done) | copy-start | bytes 6291460
  148.7 2.2 %copy-start.2 = (f32[2,256,1024]{2,1,0:T(8,128)S(1)}, f32[2,256,1024]{2,1,0:T(8,128)}, u32[]{:S(2)}) copy-start(f32[2,256,1024]{2,1,0:T(8,128)} %copy.12) | copy-start | bytes 6291460
  148.7 2.5 %copy-start.4 = (f32[1,256,1024]{2,1,0:T(8,128)S(1)}, f32[1,256,1024]{2,1,0:T(8,128)}, u32[]{:S(2)}) copy-start(f32[1,256,1024]{2,1,0:T(8,128)} %get-tuple-element.223) | copy-start | bytes 3145732
